TPU v7x, 32 devices: a whole 2x2x4 slice. The times are simulated.
32 devices in a mesh: view: 8 (over z, core), strip: 2 (over x), orbit: 2 (over y).
Axes of the slice: x: 2, y: 2, z: 4, core: 2. Of those that a mesh axis runs over, the one named last changes fastest.
Arguments:
- features: bfloat16 [16, 8, 128, 256], P(('orbit', 'view'), 'strip'), parts along dimension 0, may hold values from -6 to 6
- cotangent: bfloat16 [16, 8, 128, 256], P(('orbit', 'view'), 'strip'), parts along dimension 0, may hold values from -6 to 6
- conv_first: bfloat16 [3, 3, 256, 256], replicated, may hold values from -0.125 to 0.125
- conv_second: bfloat16 [3, 3, 256, 256], replicated, may hold values from -0.125 to 0.125
- w_query: bfloat16 [256, 256], replicated, may hold values from -6 to 6
- w_key: bfloat16 [256, 256], replicated, may hold values from -6 to 6
- w_value: bfloat16 [256, 256], replicated, may hold values from -0.375 to 0.375
- w_out: bfloat16 [256, 256], replicated, may hold values from -0.375 to 0.375
Outputs:
- grad_features: bfloat16 [16, 8, 128, 256], P(('orbit', 'view'), 'strip'), parts along dimension 0
- conv_grads: float32 [4, 2304, 256], P('orbit', 'view'), parts along dimension 0
- attn_grads: float32 [8, 256, 256], P('orbit', 'view'), parts along dimension 0
There are 2 independent parts, one for each index of `orbit`. A program takes and returns all parts, laid end to end along the dimension named above; an argument that names none is the same for every part. Nothing has to cross between parts.
All inputs are finite; a program needn't handle non-finite values.
Results may differ from a plain program's by a relative error of at most 0.017.
Values may be sent and summed in bfloat16 or wider, within the bound.
A program may use at most 64 MiB of HBM per device.

v0:
```python
import jax
import jax.numpy as jnp
from jax import lax
from jax.sharding import PartitionSpec as P


def extended(block, sides, width):
    for axis, dim in sides:
        count = lax.axis_size(axis)
        forward = [(i, i + 1) for i in range(count - 1)]
        backward = [(target, source) for source, target in forward]
        low = lax.ppermute(
            lax.slice_in_dim(block, block.shape[dim] - width, None, axis=dim), axis, forward
        )
        high = lax.ppermute(lax.slice_in_dim(block, 0, width, axis=dim), axis, backward)
        block = jnp.concatenate([low, block, high], axis=dim)
    return block


def rounded(array):
    return lax.optimization_barrier(array.astype(jnp.bfloat16))


def silu_slope(value):
    sigma = jax.nn.sigmoid(value)
    return sigma * (1.0 + value * (1.0 - sigma))


def with_rims(array):
    padded = extended(array, (("strip", 1),), 1)
    return jnp.pad(padded, ((0, 0), (0, 0), (1, 1), (0, 0)))


def flipped(kernel):
    return jnp.transpose(kernel[::-1, ::-1], (0, 1, 3, 2))


def convolve(padded, kernel):
    lead = padded.shape[0]
    rows = padded.shape[1] - 2
    cols = padded.shape[2] - 2
    chan = padded.shape[3]
    total = jnp.zeros((lead * rows * cols, kernel.shape[3]), jnp.float32)
    for shift_row in range(3):
        for shift_col in range(3):
            piece = padded[
                :, shift_row : shift_row + rows, shift_col : shift_col + cols, :
            ].reshape(-1, chan)
            total = total + jnp.dot(
                piece, kernel[shift_row, shift_col], preferred_element_type=jnp.float32
            )
    return total.reshape(lead, rows, cols, -1)


def kernel_grad(padded, upstream):
    rows = padded.shape[1] - 2
    cols = padded.shape[2] - 2
    chan = padded.shape[3]
    flat_up = upstream.reshape(-1, upstream.shape[3])
    pieces = []
    for shift_row in range(3):
        for shift_col in range(3):
            piece = padded[
                :, shift_row : shift_row + rows, shift_col : shift_col + cols, :
            ].reshape(-1, chan)
            pieces.append(
                lax.dot_general(
                    piece, flat_up, (((0,), (0,)), ((), ())), preferred_element_type=jnp.float32
                )
            )
    return jnp.stack(pieces).reshape(9 * chan, -1)


def attend(query, key, value, grad_mixed):
    chan = query.shape[-1]
    scale = chan ** (-0.5)
    scores = jnp.einsum("amc,bmc->mab", query, key, preferred_element_type=jnp.float32) * scale
    top = jnp.max(scores, axis=-1, keepdims=True)
    expo = jnp.exp(scores - top)
    prob_f = expo / jnp.sum(expo, axis=-1, keepdims=True)
    prob = prob_f.astype(jnp.bfloat16)
    mixed = jnp.einsum("mab,bmc->amc", prob, value, preferred_element_type=jnp.float32).astype(
        jnp.bfloat16
    )
    grad_prob = jnp.einsum("amc,bmc->mab", grad_mixed, value, preferred_element_type=jnp.float32)
    grad_value = jnp.einsum(
        "mab,amc->bmc", prob, grad_mixed, preferred_element_type=jnp.float32
    ).astype(jnp.bfloat16)
    inner = jnp.sum(prob_f * grad_prob, axis=-1, keepdims=True)
    grad_score = (prob_f * (grad_prob - inner) * scale).astype(jnp.bfloat16)
    grad_query = jnp.einsum(
        "mab,bmc->amc", grad_score, key, preferred_element_type=jnp.float32
    ).astype(jnp.bfloat16)
    grad_key = jnp.einsum(
        "mab,amc->bmc", grad_score, query, preferred_element_type=jnp.float32
    ).astype(jnp.bfloat16)
    return (mixed, grad_query, grad_key, grad_value)


def project(flat, weight):
    return jnp.dot(flat, weight, preferred_element_type=jnp.float32).astype(jnp.bfloat16)


def project_back(flat, weight):
    return lax.dot_general(
        flat, weight, (((1,), (1,)), ((), ())), preferred_element_type=jnp.float32
    )


def outer_sum(left, right):
    return lax.dot_general(
        left, right, (((0,), (0,)), ((), ())), preferred_element_type=jnp.float32
    )


def body(features, cotangent, conv_first, conv_second, w_query, w_key, w_value, w_out):
    chan = features.shape[3]
    pixels = features.shape[1] * features.shape[2]
    views = lax.axis_size("view")
    share = pixels // views
    inputs_f = features.astype(jnp.float32)
    act_first = jax.nn.silu(inputs_f).astype(jnp.bfloat16)
    pad_first = with_rims(act_first)
    hidden_first = rounded(convolve(pad_first, conv_first))
    act_second = jax.nn.silu(hidden_first.astype(jnp.float32)).astype(jnp.bfloat16)
    pad_second = with_rims(act_second)
    summed = rounded(inputs_f + convolve(pad_second, conv_second))
    summed_f = summed.astype(jnp.float32)
    centred = summed_f - jnp.mean(summed_f, axis=-1, keepdims=True)
    inv_scale = lax.rsqrt(jnp.mean(centred * centred, axis=-1, keepdims=True) + 1e-05)
    normed_f = centred * inv_scale
    normed = normed_f.astype(jnp.bfloat16)
    flat_normed = normed.reshape(pixels, chan)
    flat_cot = cotangent.reshape(pixels, chan)
    grad_mixed = project_back(flat_cot, w_out).astype(jnp.bfloat16)

    def to_pixels(array):
        return array.reshape(1, views, share, chan)

    def pixel_items(array):
        return array.reshape(views, share, chan)

    def to_views(array):
        return array.reshape(views, 1, share, chan)

    arrived = (
        lax.all_to_all(to_pixels(flat_normed), "view", split_axis=1, concat_axis=0, tiled=True),
        lax.all_to_all(to_pixels(grad_mixed), "view", split_axis=1, concat_axis=0, tiled=True),
    )
    normed_pix = pixel_items(arrived[0])
    grad_pix = pixel_items(arrived[1])
    rows_pix = normed_pix.reshape(-1, chan)
    query = project(rows_pix, w_query).reshape(views, share, chan)
    key = project(rows_pix, w_key).reshape(views, share, chan)
    value = project(rows_pix, w_value).reshape(views, share, chan)
    mixed, grad_query, grad_key, grad_value = attend(query, key, value, grad_pix)
    flat_gq = grad_query.reshape(-1, chan)
    flat_gk = grad_key.reshape(-1, chan)
    flat_gv = grad_value.reshape(-1, chan)
    grad_wq = outer_sum(rows_pix, flat_gq)
    grad_wk = outer_sum(rows_pix, flat_gk)
    grad_wv = outer_sum(rows_pix, flat_gv)
    back = (
        project_back(flat_gq, w_query)
        + project_back(flat_gk, w_key)
        + project_back(flat_gv, w_value)
    )
    back = back.astype(jnp.bfloat16).reshape(views, share, chan)
    returned = (
        lax.all_to_all(to_views(mixed), "view", split_axis=0, concat_axis=1, tiled=True),
        lax.all_to_all(to_views(back), "view", split_axis=0, concat_axis=1, tiled=True),
    )
    mixed_rows = returned[0].reshape(pixels, chan)
    grad_normed = returned[1].astype(jnp.float32).reshape(features.shape)
    grad_wo = outer_sum(mixed_rows, flat_cot)
    grad_summed = cotangent.astype(jnp.float32) + inv_scale * (
        grad_normed
        - jnp.mean(grad_normed, axis=-1, keepdims=True)
        - normed_f * jnp.mean(grad_normed * normed_f, axis=-1, keepdims=True)
    )
    grad_second = grad_summed.astype(jnp.bfloat16)
    slope_second = convolve(with_rims(grad_second), flipped(conv_second))
    grad_first = (slope_second * silu_slope(hidden_first.astype(jnp.float32))).astype(jnp.bfloat16)
    slope_first = convolve(with_rims(grad_first), flipped(conv_first))
    grad_features = (grad_summed + slope_first * silu_slope(inputs_f)).astype(jnp.bfloat16)
    conv_part = jnp.stack(
        [kernel_grad(pad_first, grad_first), kernel_grad(pad_second, grad_second)]
    )
    attn_part = jnp.stack([grad_wq, grad_wk, grad_wv, grad_wo])
    whole = (
        lax.psum(conv_part.astype(jnp.bfloat16), "strip").astype(jnp.float32),
        lax.psum(attn_part.astype(jnp.bfloat16), "strip").astype(jnp.float32),
    )
    conv_total, attn_total = (
        lax.psum_scatter(
            whole[0].astype(jnp.bfloat16), "view", scatter_dimension=1, tiled=True
        ).astype(jnp.float32),
        lax.psum_scatter(
            whole[1].astype(jnp.bfloat16), "view", scatter_dimension=1, tiled=True
        ).astype(jnp.float32),
    )
    return (grad_features, conv_total, attn_total)


def solution(mesh):
    return jax.shard_map(
        body,
        mesh=mesh,
        in_specs=(
            P(("orbit", "view"), "strip", None, None),
            P(("orbit", "view"), "strip", None, None),
            P(),
            P(),
            P(),
            P(),
            P(),
            P(),
        ),
        out_specs=(
            P(("orbit", "view"), "strip", None, None),
            P("orbit", "view", None),
            P("orbit", "view", None),
        ),
        check_vma=False,
    )
```

profile of v0, /device:TPU:0, one launch (start us, length us, event | category | flops | bytes accessed | tf_op | source)
XLA Modules:
  0.0 246.5 jit_solution(17187515369203246821)
XLA Ops:
  7.2 1.2 copy.123
  8.5 4.9 %collective-permute-start = (bf16[1,1,128,256]{2,3,1,0:T(8,128)(2,1)S(1)}, bf16[1,1,128,256]{2,3,1,0:T(8,128)(2,1)S(1)}, u32[]{:S(2)}, u32[]{:S(2)}) collective-permute-start(bf16[1,1,128,256]{2,3,1,0:T(8,128)(2,1)S(1)} %get-tuple-element.52), channel_id=1, source_target_pairs={{0,2},{1,3},{4,6},{5,7},{8,10},{9,11},{12,14},{13,15},{16,18},{17,... | collective-permute-start | bytes 196616 | tf_op jit(solution)/shard_map/ppermute | solution.py:12
  13.4 1.3 collective-permute-start.1
  15.6 4.0 %collective-permute-done.1 = bf16[1,1,128,256]{2,3,1,0:T(8,128)(2,1)S(1)} collective-permute-done((bf16[1,1,128,256]{2,3,1,0:T(8,128)(2,1)S(1)}, bf16[1,1,128,256]{2,3,1,0:T(8,128)(2,1)S(1)}, u32[]{:S(2)}, u32[]{:S(2)}) %collective-permute-start.1) | collective-permute-done | bytes 65568 | tf_op jit(solution)/shard_map/ppermute | solution.py:15
  24.5 1.9 copy.129
  29.2 1.2 convolution_add_fusion.33
  34.3 1.1 copy.133
  35.6 1.6 collective-permute-start.2
  37.2 1.3 collective-permute-start.3
  39.3 4.0 %collective-permute-done.3 = bf16[1,1,128,256]{2,3,1,0:T(8,128)(2,1)S(1)} collective-permute-done((bf16[1,1,128,256]{2,3,1,0:T(8,128)(2,1)S(1)}, bf16[1,1,128,256]{2,3,1,0:T(8,128)(2,1)S(1)}, u32[]{:S(2)}, u32[]{:S(2)}) %collective-permute-start.3) | collective-permute-done | bytes 65568 | tf_op jit(solution)/shard_map/ppermute | solution.py:15
  44.6 1.4 fusion.223
  47.1 1.8 copy.136
  48.9 1.8 copy.137
  50.7 1.8 copy.139
  52.5 1.8 copy.140
  55.4 1.2 fusion.168
  56.6 1.2 convolution_add_fusion.25
  61.3 1.2 copy.143
  63.7 4.9 %all-to-all-start = ((bf16[1,8,64,256]{3,2,0,1:T(8,128)(2,1)}), bf16[1,8,64,256]{3,2,0,1:T(8,128)(2,1)S(1)}, u32[]{:S(2)}, u32[]{:S(2)}) async-start(bf16[1,8,64,256]{3,2,0,1:T(8,128)(2,1)} %bitcast.39), calls=%async_computation | async-start | bytes 524288 | tf_op jit(solution)/shard_map/all_to_all | solution.py:147
  69.5 2.4 reverse_bitcast_fusion.1
  72.9 5.4 %all-to-all-done = bf16[1,8,64,256]{3,2,0,1:T(8,128)(2,1)S(1)} async-done(((bf16[1,8,64,256]{3,2,0,1:T(8,128)(2,1)}), bf16[1,8,64,256]{3,2,0,1:T(8,128)(2,1)S(1)}, u32[]{:S(2)}, u32[]{:S(2)}) %all-to-all-start) | async-done | bytes 262176 | tf_op jit(solution)/shard_map/all_to_all | solution.py:147
  78.3 3.4 %all-to-all-start.1 = ((bf16[1,8,64,256]{3,2,0,1:T(8,128)(2,1)}), bf16[1,8,64,256]{3,2,0,1:T(8,128)(2,1)S(1)}, u32[]{:S(2)}, u32[]{:S(2)}) async-start(bf16[1,8,64,256]{3,2,0,1:T(8,128)(2,1)} %bitcast.592), calls=%async_computation.1 | async-start | bytes 524288 | tf_op jit(solution)/shard_map/all_to_all | solution.py:148
  83.9 2.9 %fusion.229 = (f32[64,8]{1,0:T(8,128)}, f32[64,8,8]{1,2,0:T(8,128)}) fusion(bf16[8,64,256]{2,1,0:T(8,128)(2,1)} %bitcast.627, bf16[8,64,256]{2,1,0:T(8,128)(2,1)} %bitcast.629), kind=kOutput, calls=%fused_computation.344 | convolution fusion | flops 2109447 | bytes 542720 | tf_op jit(solution)/shard_map/sub | solution.py:79
  86.7 4.6 %all-to-all-done.1 = bf16[1,8,64,256]{3,2,0,1:T(8,128)(2,1)S(1)} async-done(((bf16[1,8,64,256]{3,2,0,1:T(8,128)(2,1)}), bf16[1,8,64,256]{3,2,0,1:T(8,128)(2,1)S(1)}, u32[]{:S(2)}, u32[]{:S(2)}) %all-to-all-start.1) | async-done | bytes 262176 | tf_op jit(solution)/shard_map/all_to_all | solution.py:148
  91.4 1.1 fusion.147
  92.5 2.4 fusion.7
  94.9 2.5 fusion.6
  97.4 1.3 fusion.8
  100.5 3.6 %all-to-all-start.2 = ((bf16[8,1,64,256]{3,2,1,0:T(8,128)(2,1)}), bf16[8,1,64,256]{3,2,1,0:T(8,128)(2,1)S(1)}, u32[]{:S(2)}, u32[]{:S(2)}) async-start(bf16[8,1,64,256]{3,2,1,0:T(8,128)(2,1)} %bitcast.620), calls=%async_computation.2 | async-start | bytes 524288 | tf_op jit(solution)/shard_map/all_to_all | solution.py:171
  104.1 1.4 fusion.9
  107.7 5.8 %all-to-all-done.2 = bf16[8,1,64,256]{3,2,1,0:T(8,128)(2,1)S(1)} async-done(((bf16[8,1,64,256]{3,2,1,0:T(8,128)(2,1)}), bf16[8,1,64,256]{3,2,1,0:T(8,128)(2,1)S(1)}, u32[]{:S(2)}, u32[]{:S(2)}) %all-to-all-start.2) | async-done | bytes 262176 | tf_op jit(solution)/shard_map/all_to_all | solution.py:171
  113.5 4.0 %all-to-all-start.3 = ((bf16[8,1,64,256]{3,2,1,0:T(8,128)(2,1)}), bf16[8,1,64,256]{3,2,1,0:T(8,128)(2,1)}, u32[]{:S(2)}, u32[]{:S(2)}) async-start(bf16[8,1,64,256]{3,2,1,0:T(8,128)(2,1)} %copy.201), calls=%async_computation.3 | async-start | bytes 524288 | tf_op jit(solution)/shard_map/all_to_all | solution.py:170
  118.5 1.2 copy.159
  120.1 1.1 fusion.202
  122.8 4.5 %all-to-all-done.3 = bf16[8,1,64,256]{3,2,1,0:T(8,128)(2,1)} async-done(((bf16[8,1,64,256]{3,2,1,0:T(8,128)(2,1)}), bf16[8,1,64,256]{3,2,1,0:T(8,128)(2,1)}, u32[]{:S(2)}, u32[]{:S(2)}) %all-to-all-start.3) | async-done | bytes 262176 | tf_op jit(solution)/shard_map/all_to_all | solution.py:170
  127.3 1.3 fusion.72
  128.6 1.8 pad_maximum_fusion.1
  130.5 1.6 collective-permute-start.4
  132.0 1.3 collective-permute-start.5
  133.3 1.9 fusion.48
  137.1 1.9 fusion.42
  145.5 1.4 fusion.222
  146.8 1.8 copy.161
  148.6 1.8 copy.163
  151.3 1.9 copy.166
  153.2 1.8 copy.167
  155.0 1.8 copy.168
  156.8 1.8 copy.169
  158.5 1.3 fusion.159
  159.8 1.2 convolution_add_fusion.15
  165.0 2.1 copy.170
  167.1 1.2 fusion.95
  171.4 1.6 pad_maximum_fusion
  173.1 4.7 %collective-permute-start.6 = (bf16[1,1,128,256]{2,3,1,0:T(8,128)(2,1)S(1)}, bf16[1,1,128,256]{2,3,1,0:T(8,128)(2,1)S(1)}, u32[]{:S(2)}, u32[]{:S(2)}) collective-permute-start(bf16[1,1,128,256]{2,3,1,0:T(8,128)(2,1)S(1)} %get-tuple-element.40), channel_id=1, source_target_pairs={{0,2},{1,3},{4,6},{5,7},{8,10},{9,11},{12,14},{13,15},{16,18},{17,... | collective-permute-start | bytes 196616 | tf_op jit(solution)/shard_map/ppermute | solution.py:12
  177.7 1.5 collective-permute-start.7
  179.3 1.1 reverse_bitcast_fusion
  181.3 2.7 %collective-permute-done.7 = bf16[1,1,128,256]{2,3,1,0:T(8,128)(2,1)S(1)} collective-permute-done((bf16[1,1,128,256]{2,3,1,0:T(8,128)(2,1)S(1)}, bf16[1,1,128,256]{2,3,1,0:T(8,128)(2,1)S(1)}, u32[]{:S(2)}, u32[]{:S(2)}) %collective-permute-start.7) | collective-permute-done | bytes 65568 | tf_op jit(solution)/shard_map/ppermute | solution.py:15
  185.2 1.2 fusion.221
  188.2 1.9 copy.176
  196.2 14.1 %reduce-scatter.3.cloned.1.call-done = bf16[2,288,256]{2,1,0:T(8,128)(2,1)} async-done(((bf16[2,2304,256]{2,1,0:T(8,128)(2,1)}), bf16[2,288,256]{2,1,0:T(8,128)(2,1)}) %reduce-scatter.3.cloned.1.call-update) | async-done | bytes 294928 | tf_op jit(solution)/shard_map/reduce_scatter | solution.py:195
  211.4 1.2 copy.180
  213.9 22.8 %all-reduce.7.cloned.1.call-done = (bf16[2,288,256]{2,1,0:T(8,128)(2,1)}, bf16[4,32,256]{2,1,0:T(8,128)(2,1)}) async-done(((bf16[2,288,256]{2,1,0:T(8,128)(2,1)}, bf16[4,32,256]{2,1,0:T(8,128)(2,1)}), (bf16[2,288,256]{2,1,0:T(8,128)(2,1)}, bf16[4,32,256]{2,1,0:T(8,128)(2,1)})) %all-reduce.7.cloned.1.call-update) | async-done | bytes 360464 | tf_op jit(solution)/shard_map/psum | solution.py:191
  236.7 1.8 convert_element_type.165
  238.5 1.5 convert_element_type.168
  (244 shorter events, 60.4 us)
Async XLA Ops:
  7.2 75.5 %copy-start = (bf16[256,256]{1,0:T(8,128)(2,1)S(1)}, bf16[256,256]{1,0:T(8,128)(2,1)}, u32[]{:S(2)}) copy-start(bf16[256,256]{1,0:T(8,128)(2,1)} %param.12) | copy-start | bytes 393220
  8.5 7.1 %collective-permute-start = (bf16[1,1,128,256]{2,3,1,0:T(8,128)(2,1)S(1)}, bf16[1,1,128,256]{2,3,1,0:T(8,128)(2,1)S(1)}, u32[]{:S(2)}, u32[]{:S(2)}) collective-permute-start(bf16[1,1,128,256]{2,3,1,0:T(8,128)(2,1)S(1)} %get-tuple-element.52), channel_id=1, source_target_pairs={{0,2},{1,3},{4,6},{5,7},{8,10},{9,11},{12,14},{13,15},{16,18},{17,... | collective-permute-start | bytes 196616 | tf_op jit(solution)/shard_map/ppermute | solution.py:12
  13.4 6.2 %collective-permute-start.1 = (bf16[1,1,128,256]{2,3,1,0:T(8,128)(2,1)S(1)}, bf16[1,1,128,256]{2,3,1,0:T(8,128)(2,1)S(1)}, u32[]{:S(2)}, u32[]{:S(2)}) collective-permute-start(bf16[1,1,128,256]{2,3,1,0:T(8,128)(2,1)S(1)} %get-tuple-element.53), channel_id=1, source_target_pairs={{2,0},{3,1},{6,4},{7,5},{10,8},{11,9},{14,12},{15,13},{18,16},{19,... | collective-permute-start | bytes 196616 | tf_op jit(solution)/shard_map/ppermute | solution.py:15
  21.9 1.8 copy-start.6
  24.5 4.5 %copy-start.1 = (bf16[3,3,256,256]{3,2,1,0:T(8,128)(2,1)S(1)}, bf16[3,3,256,256]{3,2,1,0:T(8,128)(2,1)}, u32[]{:S(2)}) copy-start(bf16[3,3,256,256]{3,2,1,0:T(8,128)(2,1)} %param.10) | copy-start | bytes 3538948
  24.5 4.5 %copy-start.21 = (bf16[1,4,128,256]{3,2,1,0:T(8,128)(2,1)S(1)}, bf16[1,4,128,256]{3,2,1,0:T(8,128)(2,1)}, u32[]{:S(2)}) copy-start(bf16[1,4,128,256]{3,2,1,0:T(8,128)(2,1)} %copy.124) | copy-start | bytes 786436
  29.0 1.5 copy-start.50
  29.2 1.5 copy-start.46
  30.7 1.0 copy-start.42
  31.4 1.0 copy-start.36
  32.4 1.0 copy-start.31
  35.4 3.9 %copy-start.12 = (bf16[1,4,128,256]{2,3,1,0:T(8,128)(2,1)}, bf16[1,4,128,256]{2,3,1,0:T(8,128)(2,1)S(1)}, u32[]{:S(2)}) copy-start(bf16[1,4,128,256]{2,3,1,0:T(8,128)(2,1)S(1)} %copy.133) | copy-start | bytes 786436
  35.6 3.7 %collective-permute-start.2 = (bf16[1,1,128,256]{2,3,1,0:T(8,128)(2,1)S(1)}, bf16[1,1,128,256]{2,3,1,0:T(8,128)(2,1)S(1)}, u32[]{:S(2)}, u32[]{:S(2)}) collective-permute-start(bf16[1,1,128,256]{2,3,1,0:T(8,128)(2,1)S(1)} %get-tuple-element.48), channel_id=1, source_target_pairs={{0,2},{1,3},{4,6},{5,7},{8,10},{9,11},{12,14},{13,15},{16,18},{17,... | collective-permute-start | bytes 196616 | tf_op jit(solution)/shard_map/ppermute | solution.py:12
  37.2 6.2 %collective-permute-start.3 = (bf16[1,1,128,256]{2,3,1,0:T(8,128)(2,1)S(1)}, bf16[1,1,128,256]{2,3,1,0:T(8,128)(2,1)S(1)}, u32[]{:S(2)}, u32[]{:S(2)}) collective-permute-start(bf16[1,1,128,256]{2,3,1,0:T(8,128)(2,1)S(1)} %get-tuple-element.49), channel_id=1, source_target_pairs={{2,0},{3,1},{6,4},{7,5},{10,8},{11,9},{14,12},{15,13},{18,16},{19,... | collective-permute-start | bytes 196616 | tf_op jit(solution)/shard_map/ppermute | solution.py:15
  43.4 10.9 %copy-start.10 = (bf16[1,4,128,256]{2,3,1,0:T(8,128)(2,1)}, bf16[1,4,128,256]{2,3,1,0:T(8,128)(2,1)S(1)}, u32[]{:S(2)}) copy-start(bf16[1,4,128,256]{2,3,1,0:T(8,128)(2,1)S(1)} %get-tuple-element.47) | copy-start | bytes 786436
  43.4 10.9 %copy-start.8 = (bf16[1,4,128,256]{2,3,1,0:T(8,128)(2,1)}, bf16[1,4,128,256]{2,3,1,0:T(8,128)(2,1)S(1)}, u32[]{:S(2)}) copy-start(bf16[1,4,128,256]{2,3,1,0:T(8,128)(2,1)S(1)} %get-tuple-element.46) | copy-start | bytes 786436
  55.3 2.5 %copy-start.3 = (bf16[3,3,256,256]{3,2,1,0:T(8,128)(2,1)S(1)}, bf16[3,3,256,256]{3,2,1,0:T(8,128)(2,1)}, u32[]{:S(2)}) copy-start(bf16[3,3,256,256]{3,2,1,0:T(8,128)(2,1)} %param.11) | copy-start | bytes 3538948
  55.3 2.5 %copy-start.51 = (bf16[1,4,128,256]{3,2,1,0:T(8,128)(2,1)S(1)}, bf16[1,4,128,256]{3,2,1,0:T(8,128)(2,1)}, u32[]{:S(2)}) copy-start(bf16[1,4,128,256]{3,2,1,0:T(8,128)(2,1)} %copy.136) | copy-start | bytes 786436
  56.6 1.5 copy-start.47
  58.1 1.0 copy-start.43
  58.8 1.0 copy-start.38
  59.1 1.0 copy-start.39
  62.6 6.0 %copy-start.11 = (bf16[1,4,128,256]{3,2,1,0:T(8,128)(2,1)S(1)}, bf16[1,4,128,256]{3,2,1,0:T(8,128)(2,1)}, u32[]{:S(2)}) copy-start(bf16[1,4,128,256]{3,2,1,0:T(8,128)(2,1)} %param.9) | copy-start | bytes 786436
  63.7 14.6 %all-to-all-start = ((bf16[1,8,64,256]{3,2,0,1:T(8,128)(2,1)}), bf16[1,8,64,256]{3,2,0,1:T(8,128)(2,1)S(1)}, u32[]{:S(2)}, u32[]{:S(2)}) async-start(bf16[1,8,64,256]{3,2,0,1:T(8,128)(2,1)} %bitcast.39), calls=%async_computation | async-start | bytes 524288 | tf_op jit(solution)/shard_map/all_to_all | solution.py:147
  69.5 2.4 copy-start.56
  71.9 9.8 %copy-start.53 = (bf16[256,256]{1,0:T(8,128)(2,1)S(1)}, bf16[256,256]{1,0:T(8,128)(2,1)}, u32[]{:S(2)}) copy-start(bf16[256,256]{1,0:T(8,128)(2,1)} %param.13) | copy-start | bytes 393220
  71.9 11.7 %copy-start.52 = (bf16[256,256]{1,0:T(8,128)(2,1)S(1)}, bf16[256,256]{1,0:T(8,128)(2,1)}, u32[]{:S(2)}) copy-start(bf16[256,256]{1,0:T(8,128)(2,1)} %param.14) | copy-start | bytes 393220
  78.3 13.1 %all-to-all-start.1 = ((bf16[1,8,64,256]{3,2,0,1:T(8,128)(2,1)}), bf16[1,8,64,256]{3,2,0,1:T(8,128)(2,1)S(1)}, u32[]{:S(2)}, u32[]{:S(2)}) async-start(bf16[1,8,64,256]{3,2,0,1:T(8,128)(2,1)} %bitcast.592), calls=%async_computation.1 | async-start | bytes 524288 | tf_op jit(solution)/shard_map/all_to_all | solution.py:148
  83.9 11.1 %copy-start.20 = (bf16[512,256]{1,0:T(8,128)(2,1)}, bf16[512,256]{1,0:T(8,128)(2,1)S(1)}, u32[]{:S(2)}) copy-start(bf16[512,256]{1,0:T(8,128)(2,1)S(1)} %convolution_convert_fusion.4) | copy-start | bytes 786436
  97.4 1.4 copy-start.54
  97.4 1.4 copy-start.55
  99.5 4.6 %copy-start.57 = (f32[64,8]{1,0:T(8,128)S(1)}, f32[64,8]{1,0:T(8,128)}, u32[]{:S(2)}) copy-start(f32[64,8]{1,0:T(8,128)} %get-tuple-element.54) | copy-start | bytes 6148
  100.5 13.1 %all-to-all-start.2 = ((bf16[8,1,64,256]{3,2,1,0:T(8,128)(2,1)}), bf16[8,1,64,256]{3,2,1,0:T(8,128)(2,1)S(1)}, u32[]{:S(2)}, u32[]{:S(2)}) async-start(bf16[8,1,64,256]{3,2,1,0:T(8,128)(2,1)} %bitcast.620), calls=%async_computation.2 | async-start | bytes 524288 | tf_op jit(solution)/shard_map/all_to_all | solution.py:171
  104.1 2.2 copy-start.15
  104.1 2.4 copy-start.17
  113.5 13.8 %all-to-all-start.3 = ((bf16[8,1,64,256]{3,2,1,0:T(8,128)(2,1)}), bf16[8,1,64,256]{3,2,1,0:T(8,128)(2,1)}, u32[]{:S(2)}, u32[]{:S(2)}) async-start(bf16[8,1,64,256]{3,2,1,0:T(8,128)(2,1)} %copy.201), calls=%async_computation.3 | async-start | bytes 524288 | tf_op jit(solution)/shard_map/all_to_all | solution.py:170
  117.6 78.6 %reduce-scatter.5.cloned.1.call-start = ((), (), s32[]{:S(2)}) async-start(), calls=%async_computation.7 | async-start | bytes 589824 | tf_op jit(solution)/shard_map/reduce_scatter | solution.py:198
  130.4 79.9 %reduce-scatter.3.cloned.1.call-start = ((), (), s32[]{:S(2)}) async-start(), calls=%async_computation.6 | async-start | bytes 2654208 | tf_op jit(solution)/shard_map/reduce_scatter | solution.py:195
  130.5 13.1 %collective-permute-start.4 = (bf16[1,1,128,256]{2,3,1,0:T(8,128)(2,1)}, bf16[1,1,128,256]{2,3,1,0:T(8,128)(2,1)S(1)}, u32[]{:S(2)}, u32[]{:S(2)}) collective-permute-start(bf16[1,1,128,256]{2,3,1,0:T(8,128)(2,1)} %get-tuple-element.44), channel_id=1, source_target_pairs={{0,2},{1,3},{4,6},{5,7},{8,10},{9,11},{12,14},{13,15},{16,18},{17,... | collective-permute-start | bytes 196616 | tf_op jit(solution)/shard_map/ppermute | solution.py:12
  132.0 11.5 %collective-permute-start.5 = (bf16[1,1,128,256]{2,3,1,0:T(8,128)(2,1)}, bf16[1,1,128,256]{2,3,1,0:T(8,128)(2,1)S(1)}, u32[]{:S(2)}, u32[]{:S(2)}) collective-permute-start(bf16[1,1,128,256]{2,3,1,0:T(8,128)(2,1)} %get-tuple-element.45), channel_id=1, source_target_pairs={{2,0},{3,1},{6,4},{7,5},{10,8},{11,9},{14,12},{15,13},{18,16},{19,... | collective-permute-start | bytes 196616 | tf_op jit(solution)/shard_map/ppermute | solution.py:15
  139.0 1.9 copy-start.9
  151.3 7.2 %copy-start.4 = (bf16[3,3,256,256]{2,3,1,0:T(8,128)(2,1)S(1)}, bf16[3,3,256,256]{2,3,1,0:T(8,128)(2,1)}, u32[]{:S(2)}) copy-start(bf16[3,3,256,256]{2,3,1,0:T(8,128)(2,1)} %reverse_bitcast_fusion.1) | copy-start | bytes 3538948
  158.5 2.5 %copy-start.48 = (bf16[1,4,128,256]{3,2,1,0:T(8,128)(2,1)S(1)}, bf16[1,4,128,256]{3,2,1,0:T(8,128)(2,1)}, u32[]{:S(2)}) copy-start(bf16[1,4,128,256]{3,2,1,0:T(8,128)(2,1)} %copy.163) | copy-start | bytes 786436
  159.8 1.6 copy-start.44
  161.4 1.0 copy-start.40
  165.0 2.1 copy-start.13
  165.0 3.6 %copy-start.7 = (bf16[1,4,128,256]{2,3,1,0:T(8,128)(2,1)S(1)}, bf16[1,4,128,256]{2,3,1,0:T(8,128)(2,1)}, u32[]{:S(2)}) copy-start(bf16[1,4,128,256]{2,3,1,0:T(8,128)(2,1)} %copy-done.6) | copy-start | bytes 786436
  170.1 1.3 copy-start.19
  173.0 6.3 %copy-start.2 = (bf16[3,3,256,256]{3,2,1,0:T(8,128)(2,1)S(1)}, bf16[3,3,256,256]{3,2,1,0:T(8,128)(2,1)}, u32[]{:S(2)}) copy-start(bf16[3,3,256,256]{3,2,1,0:T(8,128)(2,1)} %param.10) | copy-start | bytes 3538948
  173.0 63.7 %all-reduce.7.cloned.1.call-start = ((), (), s32[]{:S(2)}) async-start(), calls=%async_computation.8 | async-start | bytes 720896 | tf_op jit(solution)/shard_map/psum | solution.py:191
  173.1 8.2 %collective-permute-start.6 = (bf16[1,1,128,256]{2,3,1,0:T(8,128)(2,1)S(1)}, bf16[1,1,128,256]{2,3,1,0:T(8,128)(2,1)S(1)}, u32[]{:S(2)}, u32[]{:S(2)}) collective-permute-start(bf16[1,1,128,256]{2,3,1,0:T(8,128)(2,1)S(1)} %get-tuple-element.40), channel_id=1, source_target_pairs={{0,2},{1,3},{4,6},{5,7},{8,10},{9,11},{12,14},{13,15},{16,18},{17,... | collective-permute-start | bytes 196616 | tf_op jit(solution)/shard_map/ppermute | solution.py:12
  177.7 6.2 %collective-permute-start.7 = (bf16[1,1,128,256]{2,3,1,0:T(8,128)(2,1)S(1)}, bf16[1,1,128,256]{2,3,1,0:T(8,128)(2,1)S(1)}, u32[]{:S(2)}, u32[]{:S(2)}) collective-permute-start(bf16[1,1,128,256]{2,3,1,0:T(8,128)(2,1)S(1)} %get-tuple-element.41), channel_id=1, source_target_pairs={{2,0},{3,1},{6,4},{7,5},{10,8},{11,9},{14,12},{15,13},{18,16},{19,... | collective-permute-start | bytes 196616 | tf_op jit(solution)/shard_map/ppermute | solution.py:15
  186.4 3.7 %copy-start.23 = (bf16[1,4,128,256]{2,3,1,0:T(8,128)(2,1)S(1)}, bf16[1,4,128,256]{2,3,1,0:T(8,128)(2,1)}, u32[]{:S(2)}) copy-start(bf16[1,4,128,256]{2,3,1,0:T(8,128)(2,1)} %get-tuple-element.15) | copy-start | bytes 786436
  187.4 4.4 %copy-start.22 = (bf16[1,4,128,256]{2,3,1,0:T(8,128)(2,1)S(1)}, bf16[1,4,128,256]{2,3,1,0:T(8,128)(2,1)}, u32[]{:S(2)}) copy-start(bf16[1,4,128,256]{2,3,1,0:T(8,128)(2,1)} %get-tuple-element.14) | copy-start | bytes 786436
  188.2 4.4 %copy-start.5 = (bf16[3,3,256,256]{2,3,1,0:T(8,128)(2,1)S(1)}, bf16[3,3,256,256]{2,3,1,0:T(8,128)(2,1)}, u32[]{:S(2)}) copy-start(bf16[3,3,256,256]{2,3,1,0:T(8,128)(2,1)} %reverse_bitcast_fusion) | copy-start | bytes 3538948
  191.8 1.1 copy-start.29
  192.7 1.0 copy-start.49
  192.9 1.0 copy-start.45
  193.6 1.0 copy-start.25
  193.9 1.0 copy-start.41
  194.6 1.0 copy-start.34
  194.9 1.0 copy-start.35
  195.8 14.5 %copy-start.28 = (bf16[1,4,128,256]{3,2,1,0:T(8,128)(2,1)S(1)}, bf16[1,4,128,256]{3,2,1,0:T(8,128)(2,1)}, u32[]{:S(2)}) copy-start(bf16[1,4,128,256]{3,2,1,0:T(8,128)(2,1)} %copy.179) | copy-start | bytes 786436
  210.3 2.3 copy-start.18
  (9 other events, 8.2 us)
Sparse Core Ops, SparseCore 0:
  130.5 29.1 reduce-scatter.4
  173.1 37.1 reduce-scatter.2
  212.7 23.9 all-reduce.6
where the time goes:
time: 249 us; the launch traced here: 247 us
  waiting for transfers between devices  68.1 us (27%)
  local copies, waits for them, and re-layouts  67.7 us (27%)
  matrix products  48.3 us (19%)
  starting transfers between devices  34.1 us (14%)
  between operations  14.8 us (6%)
  other arithmetic  13.5 us (5%)
    slice x36, local copies, waits for them, and re-layouts, convolve(): padded[:, shift_row:shift_row + rows, shift_col:shift_col + cols, :]  42.7 us
    psum x1, waiting for transfers between devices, body(): lax.psum(conv_part.astype(jnp.bfloat16), 'strip').astype(jnp.float32)  22.8 us
    dot_general x36, matrix products, convolve(): jnp.dot(piece, kernel[shift_row, shift_col], preferred_element_type=jnp.f...  16.8 us
    reduce_scatter x1, waiting for transfers between devices, body(): lax.psum_scatter(whole[0].astype(jnp.bfloat16), 'view', scatter_dimension...  14.1 us
    dot_general x18, matrix products, kernel_grad(): lax.dot_general(piece, flat_up, (((0,), (0,)), ((), ())), preferred_eleme...  12.7 us
    ppermute x4, starting transfers between devices, extended(): lax.ppermute(lax.slice_in_dim(block, block.shape[dim] - width, None, axis...  12.7 us
    ppermute x4, waiting for transfers between devices, extended(): lax.ppermute(lax.slice_in_dim(block, 0, width, axis=dim), axis, backward)  10.7 us
    unnamed x119, local copies, waits for them, and re-layouts  8.58 us
  transfers between devices with their start and end apart: 15, of which 9 were waited for; matrix products, arithmetic and copies ran while one was open for 30% of the time, Pallas kernels for 0%

commit v1 on v0

--- a/solution.py
+++ b/solution.py
@@ -188,7 +188,9 @@
     )
     attn_part = jnp.stack([grad_wq, grad_wk, grad_wv, grad_wo])
     whole = (
-        lax.psum(conv_part.astype(jnp.bfloat16), "strip").astype(jnp.float32),
+        jnp.sum(lax.all_gather(conv_part.astype(jnp.bfloat16), "strip"), axis=0).astype(
+            jnp.float32
+        ),
         lax.psum(attn_part.astype(jnp.bfloat16), "strip").astype(jnp.float32),
     )
     conv_total, attn_total = (

time: 249 us -> 289 us (1.16)
  waiting for transfers between devices: 68.1 us -> 105 us
  other arithmetic: 13.5 us -> 17.7 us
    all_gather x0 -> x1, waiting for transfers between devices: none -> 62 us  [body(): lax.all_gather(conv_part.astype(jnp.bfloat16), 'strip')]
    psum x1, waiting for transfers between devices: 22.8 us -> 0.01 us  [body(): lax.psum(attn_part.astype(jnp.bfloat16), 'strip').astype(jnp.float32)]
    reduce_sum x0 -> x1, other arithmetic: none -> 5.16 us  [body(): jnp.sum(lax.all_gather(conv_part.astype(jnp.bfloat16), 'strip'), axis=0)]
    reduce_scatter x1, waiting for transfers between devices: 14.1 us -> 10.4 us  [body(): lax.psum_scatter(whole[0].astype(jnp.bfloat16), 'view', scatter_dimension...]
  transfers between devices with their start and end apart: 15 -> 16, of which waited for: 9 -> 9; matrix products, arithmetic and copies ran while one was open for 30% -> 28% of each run, Pallas kernels for 0% -> 0%
where the time goes in v1:
time: 289 us; the launch traced here: 287 us
  waiting for transfers between devices  105 us (36%)
  local copies, waits for them, and re-layouts  67.9 us (23%)
  matrix products  48.5 us (17%)
  starting transfers between devices  31.9 us (11%)
  other arithmetic  17.7 us (6%)
  between operations  16.6 us (6%)
    all_gather x1, waiting for transfers between devices, body(): lax.all_gather(conv_part.astype(jnp.bfloat16), 'strip')  62 us
    slice x36, local copies, waits for them, and re-layouts, convolve(): padded[:, shift_row:shift_row + rows, shift_col:shift_col + cols, :]  42.8 us
    dot_general x36, matrix products, convolve(): jnp.dot(piece, kernel[shift_row, shift_col], preferred_element_type=jnp.f...  17.8 us
    dot_general x18, matrix products, kernel_grad(): lax.dot_general(piece, flat_up, (((0,), (0,)), ((), ())), preferred_eleme...  12.7 us
    ppermute x4, waiting for transfers between devices, extended(): lax.ppermute(lax.slice_in_dim(block, 0, width, axis=dim), axis, backward)  10.6 us
    ppermute x4, starting transfers between devices, extended(): lax.ppermute(lax.slice_in_dim(block, block.shape[dim] - width, None, axis...  10.4 us
    reduce_scatter x1, waiting for transfers between devices, body(): lax.psum_scatter(whole[0].astype(jnp.bfloat16), 'view', scatter_dimension...  10.4 us
    unnamed x119, local copies, waits for them, and re-layouts  8.58 us
  transfers between devices with their start and end apart: 16, of which 9 were waited for; matrix products, arithmetic and copies ran while one was open for 28% of the time, Pallas kernels for 0%

profile of v1, /device:TPU:0, one launch (start us, length us, event | category | flops | bytes accessed | tf_op | source)
XLA Modules:
  0.0 287.2 jit_solution(7438295432187180636)
XLA Ops:
  8.0 1.2 copy.123
  9.3 4.9 %collective-permute-start = (bf16[1,1,128,256]{2,3,1,0:T(8,128)(2,1)S(1)}, bf16[1,1,128,256]{2,3,1,0:T(8,128)(2,1)S(1)}, u32[]{:S(2)}, u32[]{:S(2)}) collective-permute-start(bf16[1,1,128,256]{2,3,1,0:T(8,128)(2,1)S(1)} %get-tuple-element.50), channel_id=1, source_target_pairs={{0,2},{1,3},{4,6},{5,7},{8,10},{9,11},{12,14},{13,15},{16,18},{17,... | collective-permute-start | bytes 196616 | tf_op jit(solution)/shard_map/ppermute | solution.py:12
  14.2 1.3 collective-permute-start.1
  16.4 4.0 %collective-permute-done.1 = bf16[1,1,128,256]{2,3,1,0:T(8,128)(2,1)S(1)} collective-permute-done((bf16[1,1,128,256]{2,3,1,0:T(8,128)(2,1)S(1)}, bf16[1,1,128,256]{2,3,1,0:T(8,128)(2,1)S(1)}, u32[]{:S(2)}, u32[]{:S(2)}) %collective-permute-start.1) | collective-permute-done | bytes 65568 | tf_op jit(solution)/shard_map/ppermute | solution.py:15
  25.3 1.9 copy.129
  30.0 1.2 convolution_add_fusion.33
  35.1 1.1 copy.133
  36.4 1.6 collective-permute-start.2
  38.0 1.3 collective-permute-start.3
  40.2 4.0 %collective-permute-done.3 = bf16[1,1,128,256]{2,3,1,0:T(8,128)(2,1)S(1)} collective-permute-done((bf16[1,1,128,256]{2,3,1,0:T(8,128)(2,1)S(1)}, bf16[1,1,128,256]{2,3,1,0:T(8,128)(2,1)S(1)}, u32[]{:S(2)}, u32[]{:S(2)}) %collective-permute-start.3) | collective-permute-done | bytes 65568 | tf_op jit(solution)/shard_map/ppermute | solution.py:15
  45.5 1.4 fusion.223
  48.0 1.8 copy.136
  49.8 1.8 copy.137
  51.6 1.8 copy.139
  53.4 1.8 copy.140
  56.2 1.2 fusion.168
  57.5 1.3 convolution_add_fusion.25
  62.2 1.2 copy.143
  64.6 4.9 %all-to-all-start = ((bf16[1,8,64,256]{3,2,0,1:T(8,128)(2,1)}), bf16[1,8,64,256]{3,2,0,1:T(8,128)(2,1)S(1)}, u32[]{:S(2)}, u32[]{:S(2)}) async-start(bf16[1,8,64,256]{3,2,0,1:T(8,128)(2,1)} %bitcast.39), calls=%async_computation | async-start | bytes 524288 | tf_op jit(solution)/shard_map/all_to_all | solution.py:147
  70.3 2.5 reverse_bitcast_fusion.1
  73.8 5.4 %all-to-all-done = bf16[1,8,64,256]{3,2,0,1:T(8,128)(2,1)S(1)} async-done(((bf16[1,8,64,256]{3,2,0,1:T(8,128)(2,1)}), bf16[1,8,64,256]{3,2,0,1:T(8,128)(2,1)S(1)}, u32[]{:S(2)}, u32[]{:S(2)}) %all-to-all-start) | async-done | bytes 262176 | tf_op jit(solution)/shard_map/all_to_all | solution.py:147
  79.2 3.4 %all-to-all-start.1 = ((bf16[1,8,64,256]{3,2,0,1:T(8,128)(2,1)}), bf16[1,8,64,256]{3,2,0,1:T(8,128)(2,1)S(1)}, u32[]{:S(2)}, u32[]{:S(2)}) async-start(bf16[1,8,64,256]{3,2,0,1:T(8,128)(2,1)} %bitcast.592), calls=%async_computation.1 | async-start | bytes 524288 | tf_op jit(solution)/shard_map/all_to_all | solution.py:148
  84.8 2.9 fusion.229
  87.6 4.6 %all-to-all-done.1 = bf16[1,8,64,256]{3,2,0,1:T(8,128)(2,1)S(1)} async-done(((bf16[1,8,64,256]{3,2,0,1:T(8,128)(2,1)}), bf16[1,8,64,256]{3,2,0,1:T(8,128)(2,1)S(1)}, u32[]{:S(2)}, u32[]{:S(2)}) %all-to-all-start.1) | async-done | bytes 262176 | tf_op jit(solution)/shard_map/all_to_all | solution.py:148
  93.4 2.3 fusion.7
  95.7 2.4 fusion.6
  98.1 1.3 fusion.8
  101.2 3.6 %all-to-all-start.2 = ((bf16[8,1,64,256]{3,2,1,0:T(8,128)(2,1)}), bf16[8,1,64,256]{3,2,1,0:T(8,128)(2,1)S(1)}, u32[]{:S(2)}, u32[]{:S(2)}) async-start(bf16[8,1,64,256]{3,2,1,0:T(8,128)(2,1)} %bitcast.620), calls=%async_computation.2 | async-start | bytes 524288 | tf_op jit(solution)/shard_map/all_to_all | solution.py:171
  104.8 1.4 fusion.9
  107.8 6.4 %all-to-all-done.2 = bf16[8,1,64,256]{3,2,1,0:T(8,128)(2,1)S(1)} async-done(((bf16[8,1,64,256]{3,2,1,0:T(8,128)(2,1)}), bf16[8,1,64,256]{3,2,1,0:T(8,128)(2,1)S(1)}, u32[]{:S(2)}, u32[]{:S(2)}) %all-to-all-start.2) | async-done | bytes 262176 | tf_op jit(solution)/shard_map/all_to_all | solution.py:171
  114.3 4.0 %all-to-all-start.3 = ((bf16[8,1,64,256]{3,2,1,0:T(8,128)(2,1)}), bf16[8,1,64,256]{3,2,1,0:T(8,128)(2,1)}, u32[]{:S(2)}, u32[]{:S(2)}) async-start(bf16[8,1,64,256]{3,2,1,0:T(8,128)(2,1)} %copy.201), calls=%async_computation.4 | async-start | bytes 524288 | tf_op jit(solution)/shard_map/all_to_all | solution.py:170
  119.2 1.2 copy.159
  120.8 1.1 fusion.202
  123.5 4.5 %all-to-all-done.3 = bf16[8,1,64,256]{3,2,1,0:T(8,128)(2,1)} async-done(((bf16[8,1,64,256]{3,2,1,0:T(8,128)(2,1)}), bf16[8,1,64,256]{3,2,1,0:T(8,128)(2,1)}, u32[]{:S(2)}, u32[]{:S(2)}) %all-to-all-start.3) | async-done | bytes 262176 | tf_op jit(solution)/shard_map/all_to_all | solution.py:170
  128.0 1.3 fusion.72
  130.3 1.6 collective-permute-start.4
  131.9 1.3 collective-permute-start.5
  133.2 1.9 fusion.48
  136.9 1.9 fusion.42
  145.3 1.4 fusion.222
  146.7 1.8 copy.161
  148.5 1.8 copy.163
  151.1 1.9 copy.166
  153.0 1.8 copy.167
  154.8 1.8 copy.168
  156.6 1.8 copy.169
  158.4 1.2 fusion.159
  159.7 1.3 convolution_add_fusion.15
  164.9 2.1 copy.170
  167.0 1.2 fusion.95
  171.2 1.6 pad_maximum_fusion
  173.5 62.0 %all-gather.2.cloned.1.call-done = bf16[2,2,2304,256]{3,2,1,0:T(8,128)(2,1)} async-done(((bf16[1,2,2304,256]{3,2,1,0:T(8,128)(2,1)}), bf16[2,2,2304,256]{3,2,1,0:T(8,128)(2,1)}) %all-gather.2.cloned.1.call-update) | async-done | bytes 4718608 | tf_op jit(solution)/shard_map/all_gather | solution.py:191
  235.5 5.2 %reduce_sum.72 = bf16[2,2304,256]{2,1,0:T(8,128)(2,1)} reduce(bf16[2,2,2304,256]{3,2,1,0:T(8,128)(2,1)} %all-gather.2.cloned.1.call-done, bf16[]{:T(256)} %constant.17.clone.1), dimensions={0}, to_apply=%region_7.8 | reduce | flops 1179648 | bytes 7077890 | tf_op jit(solution)/shard_map/reduce_sum | solution.py:191
  240.7 2.4 collective-permute-start.6
  243.2 1.5 collective-permute-start.7
  244.7 1.2 reverse_bitcast_fusion
  246.7 2.6 collective-permute-done.7
  250.6 1.2 fusion.221
  253.6 1.9 copy.176
  258.4 1.2 convolution_add_fusion.7
  263.6 1.2 copy.180
  266.1 1.5 convert_element_type.177
  267.6 10.4 %reduce-scatter.3.cloned.1.call-done = bf16[2,288,256]{2,1,0:T(8,128)(2,1)} async-done(((bf16[2,2304,256]{2,1,0:T(8,128)(2,1)}), bf16[2,288,256]{2,1,0:T(8,128)(2,1)}) %reduce-scatter.3.cloned.1.call-update) | async-done | bytes 294928 | tf_op jit(solution)/shard_map/reduce_scatter | solution.py:197
  278.0 1.8 convert_element_type.174
  (248 shorter events, 62.2 us)
Async XLA Ops:
  8.0 75.6 %copy-start = (bf16[256,256]{1,0:T(8,128)(2,1)S(1)}, bf16[256,256]{1,0:T(8,128)(2,1)}, u32[]{:S(2)}) copy-start(bf16[256,256]{1,0:T(8,128)(2,1)} %param.12) | copy-start | bytes 393220
  9.3 7.1 %collective-permute-start = (bf16[1,1,128,256]{2,3,1,0:T(8,128)(2,1)S(1)}, bf16[1,1,128,256]{2,3,1,0:T(8,128)(2,1)S(1)}, u32[]{:S(2)}, u32[]{:S(2)}) collective-permute-start(bf16[1,1,128,256]{2,3,1,0:T(8,128)(2,1)S(1)} %get-tuple-element.50), channel_id=1, source_target_pairs={{0,2},{1,3},{4,6},{5,7},{8,10},{9,11},{12,14},{13,15},{16,18},{17,... | collective-permute-start | bytes 196616 | tf_op jit(solution)/shard_map/ppermute | solution.py:12
  14.2 6.2 %collective-permute-start.1 = (bf16[1,1,128,256]{2,3,1,0:T(8,128)(2,1)S(1)}, bf16[1,1,128,256]{2,3,1,0:T(8,128)(2,1)S(1)}, u32[]{:S(2)}, u32[]{:S(2)}) collective-permute-start(bf16[1,1,128,256]{2,3,1,0:T(8,128)(2,1)S(1)} %get-tuple-element.51), channel_id=1, source_target_pairs={{2,0},{3,1},{6,4},{7,5},{10,8},{11,9},{14,12},{15,13},{18,16},{19,... | collective-permute-start | bytes 196616 | tf_op jit(solution)/shard_map/ppermute | solution.py:15
  22.7 1.7 copy-start.7
  25.3 4.5 %copy-start.2 = (bf16[3,3,256,256]{3,2,1,0:T(8,128)(2,1)S(1)}, bf16[3,3,256,256]{3,2,1,0:T(8,128)(2,1)}, u32[]{:S(2)}) copy-start(bf16[3,3,256,256]{3,2,1,0:T(8,128)(2,1)} %param.10) | copy-start | bytes 3538948
  25.3 4.5 %copy-start.22 = (bf16[1,4,128,256]{3,2,1,0:T(8,128)(2,1)S(1)}, bf16[1,4,128,256]{3,2,1,0:T(8,128)(2,1)}, u32[]{:S(2)}) copy-start(bf16[1,4,128,256]{3,2,1,0:T(8,128)(2,1)} %copy.124) | copy-start | bytes 786436
  29.8 1.5 copy-start.50
  30.0 1.5 copy-start.46
  31.5 1.0 copy-start.42
  32.2 1.0 copy-start.36
  32.5 1.0 copy-start.37
  33.2 1.0 copy-start.31
  36.2 3.9 %copy-start.13 = (bf16[1,4,128,256]{2,3,1,0:T(8,128)(2,1)}, bf16[1,4,128,256]{2,3,1,0:T(8,128)(2,1)S(1)}, u32[]{:S(2)}) copy-start(bf16[1,4,128,256]{2,3,1,0:T(8,128)(2,1)S(1)} %copy.133) | copy-start | bytes 786436
  36.4 3.7 %collective-permute-start.2 = (bf16[1,1,128,256]{2,3,1,0:T(8,128)(2,1)S(1)}, bf16[1,1,128,256]{2,3,1,0:T(8,128)(2,1)S(1)}, u32[]{:S(2)}, u32[]{:S(2)}) collective-permute-start(bf16[1,1,128,256]{2,3,1,0:T(8,128)(2,1)S(1)} %get-tuple-element.46), channel_id=1, source_target_pairs={{0,2},{1,3},{4,6},{5,7},{8,10},{9,11},{12,14},{13,15},{16,18},{17,... | collective-permute-start | bytes 196616 | tf_op jit(solution)/shard_map/ppermute | solution.py:12
  38.0 6.2 %collective-permute-start.3 = (bf16[1,1,128,256]{2,3,1,0:T(8,128)(2,1)S(1)}, bf16[1,1,128,256]{2,3,1,0:T(8,128)(2,1)S(1)}, u32[]{:S(2)}, u32[]{:S(2)}) collective-permute-start(bf16[1,1,128,256]{2,3,1,0:T(8,128)(2,1)S(1)} %get-tuple-element.47), channel_id=1, source_target_pairs={{2,0},{3,1},{6,4},{7,5},{10,8},{11,9},{14,12},{15,13},{18,16},{19,... | collective-permute-start | bytes 196616 | tf_op jit(solution)/shard_map/ppermute | solution.py:15
  44.2 11.0 %copy-start.11 = (bf16[1,4,128,256]{2,3,1,0:T(8,128)(2,1)}, bf16[1,4,128,256]{2,3,1,0:T(8,128)(2,1)S(1)}, u32[]{:S(2)}) copy-start(bf16[1,4,128,256]{2,3,1,0:T(8,128)(2,1)S(1)} %get-tuple-element.45) | copy-start | bytes 786436
  44.2 11.0 %copy-start.9 = (bf16[1,4,128,256]{2,3,1,0:T(8,128)(2,1)}, bf16[1,4,128,256]{2,3,1,0:T(8,128)(2,1)S(1)}, u32[]{:S(2)}) copy-start(bf16[1,4,128,256]{2,3,1,0:T(8,128)(2,1)S(1)} %get-tuple-element.44) | copy-start | bytes 786436
  56.2 2.5 copy-start.4
  56.2 2.5 copy-start.51
  57.5 1.5 copy-start.47
  59.0 1.0 copy-start.43
  59.7 1.0 copy-start.38
  63.5 6.0 %copy-start.12 = (bf16[1,4,128,256]{3,2,1,0:T(8,128)(2,1)S(1)}, bf16[1,4,128,256]{3,2,1,0:T(8,128)(2,1)}, u32[]{:S(2)}) copy-start(bf16[1,4,128,256]{3,2,1,0:T(8,128)(2,1)} %param.9) | copy-start | bytes 786436
  64.6 14.6 %all-to-all-start = ((bf16[1,8,64,256]{3,2,0,1:T(8,128)(2,1)}), bf16[1,8,64,256]{3,2,0,1:T(8,128)(2,1)S(1)}, u32[]{:S(2)}, u32[]{:S(2)}) async-start(bf16[1,8,64,256]{3,2,0,1:T(8,128)(2,1)} %bitcast.39), calls=%async_computation | async-start | bytes 524288 | tf_op jit(solution)/shard_map/all_to_all | solution.py:147
  70.3 2.5 copy-start.56
  72.8 9.8 %copy-start.53 = (bf16[256,256]{1,0:T(8,128)(2,1)S(1)}, bf16[256,256]{1,0:T(8,128)(2,1)}, u32[]{:S(2)}) copy-start(bf16[256,256]{1,0:T(8,128)(2,1)} %param.13) | copy-start | bytes 393220
  72.8 11.7 %copy-start.52 = (bf16[256,256]{1,0:T(8,128)(2,1)S(1)}, bf16[256,256]{1,0:T(8,128)(2,1)}, u32[]{:S(2)}) copy-start(bf16[256,256]{1,0:T(8,128)(2,1)} %param.14) | copy-start | bytes 393220
  79.2 13.1 %all-to-all-start.1 = ((bf16[1,8,64,256]{3,2,0,1:T(8,128)(2,1)}), bf16[1,8,64,256]{3,2,0,1:T(8,128)(2,1)S(1)}, u32[]{:S(2)}, u32[]{:S(2)}) async-start(bf16[1,8,64,256]{3,2,0,1:T(8,128)(2,1)} %bitcast.592), calls=%async_computation.1 | async-start | bytes 524288 | tf_op jit(solution)/shard_map/all_to_all | solution.py:148
  84.8 10.9 %copy-start.21 = (bf16[512,256]{1,0:T(8,128)(2,1)}, bf16[512,256]{1,0:T(8,128)(2,1)S(1)}, u32[]{:S(2)}) copy-start(bf16[512,256]{1,0:T(8,128)(2,1)S(1)} %convolution_convert_fusion.4) | copy-start | bytes 786436
  98.1 1.4 copy-start.54
  98.1 1.4 copy-start.55
  100.2 4.6 %copy-start.57 = (f32[64,8]{1,0:T(8,128)S(1)}, f32[64,8]{1,0:T(8,128)}, u32[]{:S(2)}) copy-start(f32[64,8]{1,0:T(8,128)} %get-tuple-element.52) | copy-start | bytes 6148
  101.2 13.1 %all-to-all-start.2 = ((bf16[8,1,64,256]{3,2,1,0:T(8,128)(2,1)}), bf16[8,1,64,256]{3,2,1,0:T(8,128)(2,1)S(1)}, u32[]{:S(2)}, u32[]{:S(2)}) async-start(bf16[8,1,64,256]{3,2,1,0:T(8,128)(2,1)} %bitcast.620), calls=%async_computation.2 | async-start | bytes 524288 | tf_op jit(solution)/shard_map/all_to_all | solution.py:171
  104.8 2.2 copy-start.16
  104.8 2.4 copy-start.18
  114.3 13.8 %all-to-all-start.3 = ((bf16[8,1,64,256]{3,2,1,0:T(8,128)(2,1)}), bf16[8,1,64,256]{3,2,1,0:T(8,128)(2,1)}, u32[]{:S(2)}, u32[]{:S(2)}) async-start(bf16[8,1,64,256]{3,2,1,0:T(8,128)(2,1)} %copy.201), calls=%async_computation.4 | async-start | bytes 524288 | tf_op jit(solution)/shard_map/all_to_all | solution.py:170
  118.3 54.6 %reduce-scatter.5.cloned.1.call-start = ((), (), s32[]{:S(2)}) async-start(), calls=%async_computation.8 | async-start | bytes 589824 | tf_op jit(solution)/shard_map/reduce_scatter | solution.py:200
  130.2 105.3 %all-gather.2.cloned.1.call-start = ((), (), s32[]{:S(2)}) async-start(), calls=%async_computation.6 | async-start | bytes 7077888 | tf_op jit(solution)/shard_map/all_gather | solution.py:191
  130.3 13.0 %collective-permute-start.4 = (bf16[1,1,128,256]{2,3,1,0:T(8,128)(2,1)}, bf16[1,1,128,256]{2,3,1,0:T(8,128)(2,1)S(1)}, u32[]{:S(2)}, u32[]{:S(2)}) collective-permute-start(bf16[1,1,128,256]{2,3,1,0:T(8,128)(2,1)} %get-tuple-element.42), channel_id=1, source_target_pairs={{0,2},{1,3},{4,6},{5,7},{8,10},{9,11},{12,14},{13,15},{16,18},{17,... | collective-permute-start | bytes 196616 | tf_op jit(solution)/shard_map/ppermute | solution.py:12
  131.9 11.5 %collective-permute-start.5 = (bf16[1,1,128,256]{2,3,1,0:T(8,128)(2,1)}, bf16[1,1,128,256]{2,3,1,0:T(8,128)(2,1)S(1)}, u32[]{:S(2)}, u32[]{:S(2)}) collective-permute-start(bf16[1,1,128,256]{2,3,1,0:T(8,128)(2,1)} %get-tuple-element.43), channel_id=1, source_target_pairs={{2,0},{3,1},{6,4},{7,5},{10,8},{11,9},{14,12},{15,13},{18,16},{19,... | collective-permute-start | bytes 196616 | tf_op jit(solution)/shard_map/ppermute | solution.py:15
  138.8 1.9 copy-start.10
  151.1 7.3 %copy-start.5 = (bf16[3,3,256,256]{2,3,1,0:T(8,128)(2,1)S(1)}, bf16[3,3,256,256]{2,3,1,0:T(8,128)(2,1)}, u32[]{:S(2)}) copy-start(bf16[3,3,256,256]{2,3,1,0:T(8,128)(2,1)} %reverse_bitcast_fusion.1) | copy-start | bytes 3538948
  158.4 2.5 copy-start.48
  159.7 1.6 copy-start.44
  161.2 1.0 copy-start.40
  164.9 2.1 copy-start.14
  164.9 3.6 %copy-start.8 = (bf16[1,4,128,256]{2,3,1,0:T(8,128)(2,1)S(1)}, bf16[1,4,128,256]{2,3,1,0:T(8,128)(2,1)}, u32[]{:S(2)}) copy-start(bf16[1,4,128,256]{2,3,1,0:T(8,128)(2,1)} %copy-done.7) | copy-start | bytes 786436
  170.0 1.3 copy-start.20
  172.9 93.2 %all-reduce.6.cloned.1.call-start = ((), (), s32[]{:S(2)}) async-start(), calls=%async_computation.9 | async-start | bytes 131072 | tf_op jit(solution)/shard_map/psum | solution.py:194
  173.5 104.5 %reduce-scatter.3.cloned.1.call-start = ((), (), s32[]{:S(2)}) async-start(), calls=%async_computation.7 | async-start | bytes 2654208 | tf_op jit(solution)/shard_map/reduce_scatter | solution.py:197
  240.7 4.0 %copy-start.3 = (bf16[3,3,256,256]{3,2,1,0:T(8,128)(2,1)S(1)}, bf16[3,3,256,256]{3,2,1,0:T(8,128)(2,1)}, u32[]{:S(2)}) copy-start(bf16[3,3,256,256]{3,2,1,0:T(8,128)(2,1)} %param.10) | copy-start | bytes 3538948
  240.7 6.0 %collective-permute-start.6 = (bf16[1,1,128,256]{2,3,1,0:T(8,128)(2,1)S(1)}, bf16[1,1,128,256]{2,3,1,0:T(8,128)(2,1)S(1)}, u32[]{:S(2)}, u32[]{:S(2)}) collective-permute-start(bf16[1,1,128,256]{2,3,1,0:T(8,128)(2,1)S(1)} %get-tuple-element.38), channel_id=1, source_target_pairs={{0,2},{1,3},{4,6},{5,7},{8,10},{9,11},{12,14},{13,15},{16,18},{17,... | collective-permute-start | bytes 196616 | tf_op jit(solution)/shard_map/ppermute | solution.py:12
  243.2 6.2 %collective-permute-start.7 = (bf16[1,1,128,256]{2,3,1,0:T(8,128)(2,1)S(1)}, bf16[1,1,128,256]{2,3,1,0:T(8,128)(2,1)S(1)}, u32[]{:S(2)}, u32[]{:S(2)}) collective-permute-start(bf16[1,1,128,256]{2,3,1,0:T(8,128)(2,1)S(1)} %get-tuple-element.39), channel_id=1, source_target_pairs={{2,0},{3,1},{6,4},{7,5},{10,8},{11,9},{14,12},{15,13},{18,16},{19,... | collective-permute-start | bytes 196616 | tf_op jit(solution)/shard_map/ppermute | solution.py:15
  251.8 3.8 %copy-start.24 = (bf16[1,4,128,256]{2,3,1,0:T(8,128)(2,1)S(1)}, bf16[1,4,128,256]{2,3,1,0:T(8,128)(2,1)}, u32[]{:S(2)}) copy-start(bf16[1,4,128,256]{2,3,1,0:T(8,128)(2,1)} %get-tuple-element.13) | copy-start | bytes 786436
  252.8 4.5 %copy-start.23 = (bf16[1,4,128,256]{2,3,1,0:T(8,128)(2,1)S(1)}, bf16[1,4,128,256]{2,3,1,0:T(8,128)(2,1)}, u32[]{:S(2)}) copy-start(bf16[1,4,128,256]{2,3,1,0:T(8,128)(2,1)} %get-tuple-element.12) | copy-start | bytes 786436
  253.6 4.4 %copy-start.6 = (bf16[3,3,256,256]{2,3,1,0:T(8,128)(2,1)S(1)}, bf16[3,3,256,256]{2,3,1,0:T(8,128)(2,1)}, u32[]{:S(2)}) copy-start(bf16[3,3,256,256]{2,3,1,0:T(8,128)(2,1)} %reverse_bitcast_fusion) | copy-start | bytes 3538948
  258.1 1.5 copy-start.49
  258.4 1.6 copy-start.45
  259.9 1.0 copy-start.41
  260.6 1.0 copy-start.34
  260.9 1.0 copy-start.35
  261.6 1.0 copy-start.30
  262.5 2.3 copy-start.19
  264.8 14.9 %copy-start.1 = (bf16[256,256]{1,0:T(8,128)(2,1)S(1)}, bf16[256,256]{1,0:T(8,128)(2,1)}, u32[]{:S(2)}) copy-start(bf16[256,256]{1,0:T(8,128)(2,1)} %param.12) | copy-start | bytes 393220
  (10 other events, 9.2 us)
Sparse Core Ops, SparseCore 0:
  130.4 29.2 reduce-scatter.4
  240.8 37.0 reduce-scatter.2
Sparse Core Ops, SparseCore 1:
  172.9 62.5 all-gather.1
  237.6 20.8 all-reduce.5
